TPU v7x, 32 devices: a whole 2x2x4 slice. The times are simulated.
32 devices in a mesh: rows: 4 (over y, x), cols: 8 (over z, core).
Axes of the slice: x: 2, y: 2, z: 4, core: 2. Of those that a mesh axis runs over, the one named last changes fastest.
Arguments:
- tokens: bfloat16 [128, 256, 256], P('rows', 'cols'), may hold values from -45 to 45
- key_bias: bfloat16 [128, 256], P('rows', 'cols'), may hold values from -3 to 250
- cotangent: bfloat16 [128, 256, 256], P('rows', 'cols'), may hold values from -6 to 6
- gain_row: float32 [256], replicated, may hold values from 0.1 to 1.9
- w_qkv_row: bfloat16 [256, 768], replicated, may hold values from -0.375 to 0.375
- w_out_row: bfloat16 [256, 256], replicated, may hold values from -0.375 to 0.375
- gain_col: float32 [256], replicated, may hold values from 0.1 to 1.9
- w_qkv_col: bfloat16 [256, 768], replicated, may hold values from -0.375 to 0.375
- w_out_col: bfloat16 [256, 256], replicated, may hold values from -0.375 to 0.375
- gain_mlp: float32 [256], replicated, may hold values from 0.1 to 1.9
- w_up: bfloat16 [256, 1024], replicated, may hold values from -0.375 to 0.375
- w_down: bfloat16 [1024, 256], replicated, may hold values from -0.1875 to 0.1875
Outputs:
- d_tokens: bfloat16 [128, 256, 256], P('rows', 'cols')
- d_gain_row: float32 [256], replicated
- d_w_qkv_row: float32 [256, 768], replicated
- d_w_out_row: float32 [256, 256], replicated
- d_gain_col: float32 [256], replicated
- d_w_qkv_col: float32 [256, 768], replicated
- d_w_out_col: float32 [256, 256], replicated
- d_gain_mlp: float32 [256], replicated
- d_w_up: float32 [256, 1024], replicated
- d_w_down: float32 [1024, 256], replicated
All inputs are finite; a program needn't handle non-finite values.
Results may differ from a plain program's by a relative error of at most 0.015.
Values may be sent and summed in bfloat16 or wider, within the bound.
No kernel may reach another device: no remote copies, remote signals or barrier semaphores. Data moves between devices by JAX's collectives and lax.ppermute only.
A program may use at most 128 MiB of HBM per device.

v0:
```python
import jax
import jax.numpy as jnp
from jax import lax
from jax.sharding import PartitionSpec as P

HEADS = 4


def product(spec_text, left_op, right_op):
    return jnp.einsum(spec_text, left_op, right_op, preferred_element_type=jnp.float32)


def layer_norm(entries, gain_vec):
    floats = entries.astype(jnp.float32)
    centred = floats - jnp.mean(floats, axis=-1, keepdims=True)
    inverse = lax.rsqrt(jnp.mean(centred * centred, axis=-1, keepdims=True) + 1e-05)
    normed = centred * inverse
    return ((normed * gain_vec).astype(jnp.bfloat16), normed, inverse)


def norm_back(grad_out, normed, inverse, gain_vec):
    scaled = grad_out * gain_vec
    result = inverse * (
        scaled
        - jnp.mean(scaled, axis=-1, keepdims=True)
        - normed * jnp.mean(scaled * normed, axis=-1, keepdims=True)
    )
    gain_grad = jnp.sum((grad_out * normed).reshape(-1, gain_vec.shape[0]), axis=0)
    return (result, gain_grad)


def over_cells(left_op, right_op):
    left_flat = left_op.reshape(-1, left_op.shape[-1])
    right_flat = right_op.reshape(-1, right_op.shape[-1])
    return lax.dot_general(
        left_flat, right_flat, (((0,), (0,)), ((), ())), preferred_element_type=jnp.float32
    )


def times_transpose(entries, weight):
    return lax.dot_general(
        entries, weight, (((entries.ndim - 1,), (1,)), ((), ())), preferred_element_type=jnp.float32
    )


def letters(length_axis):
    if length_axis == 1:
        return ("sqhd,skhd->shqk", "shqk,skhd->sqhd", "shqk,sqhd->skhd")
    return ("qshd,kshd->shqk", "shqk,kshd->qshd", "shqk,qshd->kshd")


def split_heads(packed, head_count):
    features = packed.shape[-1] // 3
    head_shape = packed.shape[:-1] + (head_count, features // head_count)
    return tuple(
        (
            packed[..., member * features : (member + 1) * features].reshape(head_shape)
            for member in range(3)
        )
    )


def key_terms(bias_rows, length_axis):
    floats = bias_rows.astype(jnp.float32)
    if length_axis == 0:
        floats = floats.T
    return floats[:, None, None, :]


def attention_weights(query_block, key_rows, bias_terms, factor, length_axis):
    scores = product(letters(length_axis)[0], query_block, key_rows) * factor + bias_terms
    shifted = jnp.exp(scores - jnp.max(scores, axis=-1, keepdims=True))
    return shifted / jnp.sum(shifted, axis=-1, keepdims=True)


def join_blocks(stacked, length_axis, features):
    if length_axis == 0:
        return stacked.reshape((-1, stacked.shape[2], features))
    reordered = jnp.moveaxis(stacked, 0, 1)
    return reordered.reshape((reordered.shape[0], -1, features))


def attend(packed, bias_rows, head_count, length_axis):
    query_rows, key_rows, value_rows = split_heads(packed, head_count)
    length = packed.shape[length_axis]
    block_len = min(length, 512)
    factor = query_rows.shape[-1] ** (-0.5)
    bias_terms = key_terms(bias_rows, length_axis)
    mixing = letters(length_axis)[1]

    def one_block(offset):
        query_block = lax.dynamic_slice_in_dim(query_rows, offset, block_len, length_axis)
        weights = attention_weights(query_block, key_rows, bias_terms, factor, length_axis)
        return product(mixing, weights.astype(jnp.bfloat16), value_rows).astype(jnp.bfloat16)

    offsets = jnp.arange(length // block_len, dtype=jnp.int32) * block_len
    return join_blocks(lax.map(one_block, offsets), length_axis, packed.shape[-1] // 3)


def attend_back(grad_out, packed, bias_rows, head_count, length_axis):
    query_rows, key_rows, value_rows = split_heads(packed, head_count)
    features = packed.shape[-1] // 3
    grad_heads = grad_out.reshape(query_rows.shape)
    length = packed.shape[length_axis]
    block_len = min(length, 512)
    factor = query_rows.shape[-1] ** (-0.5)
    bias_terms = key_terms(bias_rows, length_axis)
    score_spec, mixing, gather_spec = letters(length_axis)

    def one_block(running, offset):
        key_grad, value_grad = running
        query_block = lax.dynamic_slice_in_dim(query_rows, offset, block_len, length_axis)
        grad_block = lax.dynamic_slice_in_dim(grad_heads, offset, block_len, length_axis)
        weights = attention_weights(query_block, key_rows, bias_terms, factor, length_axis)
        weights_low = weights.astype(jnp.bfloat16)
        weight_grad = product(score_spec, grad_block, value_rows)
        centre = jnp.sum(weights * weight_grad, axis=-1, keepdims=True)
        score_grad = (weights * (weight_grad - centre) * factor).astype(jnp.bfloat16)
        query_grad = product(mixing, score_grad, key_rows)
        key_grad = key_grad + product(gather_spec, score_grad, query_block)
        value_grad = value_grad + product(gather_spec, weights_low, grad_block)
        return ((key_grad, value_grad), query_grad)

    empty_grad = jnp.zeros(key_rows.shape, jnp.float32)
    offsets = jnp.arange(length // block_len, dtype=jnp.int32) * block_len
    (key_grad, value_grad), query_parts = lax.scan(one_block, (empty_grad, empty_grad), offsets)
    query_grad = join_blocks(query_parts, length_axis, features)
    flat_shape = packed.shape[:-1] + (features,)
    joined = jnp.concatenate(
        [query_grad, key_grad.reshape(flat_shape), value_grad.reshape(flat_shape)], axis=-1
    )
    return joined.astype(jnp.bfloat16)


def attention_forward(inputs, bias_rows, gain_vec, w_qkv, w_out, head_count, length_axis):
    normal_in, normed, inverse = layer_norm(inputs, gain_vec)
    packed = jnp.dot(normal_in, w_qkv, preferred_element_type=jnp.float32).astype(jnp.bfloat16)
    mixed_out = attend(packed, bias_rows, head_count, length_axis)
    output = (
        inputs.astype(jnp.float32) + jnp.dot(mixed_out, w_out, preferred_element_type=jnp.float32)
    ).astype(jnp.bfloat16)
    return (output, (normal_in, normed, inverse, packed, mixed_out))


def attention_backward(
    grad_out, saved_parts, bias_rows, gain_vec, w_qkv, w_out, head_count, length_axis
):
    normal_in, normed, inverse, packed, mixed_out = saved_parts
    out_grad = over_cells(mixed_out, grad_out)
    mixed_grad = times_transpose(grad_out, w_out).astype(jnp.bfloat16)
    packed_grad = attend_back(mixed_grad, packed, bias_rows, head_count, length_axis)
    qkv_grad = over_cells(normal_in, packed_grad)
    input_grad, gain_grad = norm_back(
        times_transpose(packed_grad, w_qkv), normed, inverse, gain_vec
    )
    return (
        (grad_out.astype(jnp.float32) + input_grad).astype(jnp.bfloat16),
        (gain_grad, qkv_grad, out_grad),
    )


def feed_backward(inputs, grad_out, gain_vec, w_up, w_down):
    normal_in, normed, inverse = layer_norm(inputs, gain_vec)
    hidden = jnp.dot(normal_in, w_up, preferred_element_type=jnp.float32)
    active, gelu_back = jax.vjp(jax.nn.gelu, hidden)
    active_low = active.astype(jnp.bfloat16)
    down_grad = over_cells(active_low, grad_out)
    hidden_grad = gelu_back(times_transpose(grad_out, w_down))[0].astype(jnp.bfloat16)
    up_grad = over_cells(normal_in, hidden_grad)
    input_grad, gain_grad = norm_back(times_transpose(hidden_grad, w_up), normed, inverse, gain_vec)
    return (
        (grad_out.astype(jnp.float32) + input_grad).astype(jnp.bfloat16),
        (gain_grad, up_grad, down_grad),
    )


def shards(
    tokens,
    key_bias,
    cotangent,
    gain_row,
    w_qkv_row,
    w_out_row,
    gain_col,
    w_qkv_col,
    w_out_col,
    gain_mlp,
    w_up,
    w_down,
):
    row_cells, row_bias = (
        lax.all_to_all(tokens, "cols", split_axis=0, concat_axis=1, tiled=True),
        lax.all_to_all(key_bias, "cols", split_axis=0, concat_axis=1, tiled=True),
    )
    after_rows, row_saved = attention_forward(
        row_cells, row_bias, gain_row, w_qkv_row, w_out_row, HEADS, 1
    )
    column_cells = lax.all_to_all(
        lax.all_to_all(after_rows, "cols", split_axis=1, concat_axis=0, tiled=True),
        "rows",
        split_axis=1,
        concat_axis=0,
        tiled=True,
    )
    column_grads, column_bias = (
        lax.all_to_all(cotangent, "rows", split_axis=1, concat_axis=0, tiled=True),
        lax.all_to_all(key_bias, "rows", split_axis=1, concat_axis=0, tiled=True),
    )
    after_cols, column_saved = attention_forward(
        column_cells, column_bias, gain_col, w_qkv_col, w_out_col, HEADS, 0
    )
    mid_grad, feed_grads = feed_backward(after_cols, column_grads, gain_mlp, w_up, w_down)
    cell_grad, attn_grads = attention_backward(
        mid_grad, column_saved, column_bias, gain_col, w_qkv_col, w_out_col, HEADS, 0
    )
    factor = float(
        tokens.shape[0] * tokens.shape[1] * lax.axis_size("rows") * lax.axis_size("cols")
    ) ** (-0.5)
    other_sums = tuple((grad_term * factor for grad_term in attn_grads + feed_grads))
    grad_rows = lax.all_to_all(
        lax.all_to_all(cell_grad, "rows", split_axis=0, concat_axis=1, tiled=True),
        "cols",
        split_axis=0,
        concat_axis=1,
        tiled=True,
    )
    token_grad_rows, row_grads = attention_backward(
        grad_rows, row_saved, row_bias, gain_row, w_qkv_row, w_out_row, HEADS, 1
    )
    d_tokens = lax.all_to_all(token_grad_rows, "cols", split_axis=1, concat_axis=0, tiled=True)
    row_sums = tuple((grad_term * factor for grad_term in row_grads))
    summed = lax.psum(
        (
            row_sums[0],
            row_sums[1],
            row_sums[2],
            other_sums[0],
            other_sums[1],
            other_sums[2],
            other_sums[3],
            other_sums[4],
            other_sums[5],
        ),
        ("rows", "cols"),
    )
    row_sums = summed[:3]
    other_sums = summed[3:]
    return (
        d_tokens,
        row_sums[0],
        row_sums[1],
        row_sums[2],
        other_sums[0],
        other_sums[1],
        other_sums[2],
        other_sums[3],
        other_sums[4],
        other_sums[5],
    )


def solution(mesh):
    in_specs = (
        P("rows", "cols", None),
        P("rows", "cols"),
        P("rows", "cols", None),
        P(),
        P(),
        P(),
        P(),
        P(),
        P(),
        P(),
        P(),
        P(),
    )
    out_specs = (P("rows", "cols", None), P(), P(), P(), P(), P(), P(), P(), P(), P())
    return jax.shard_map(shards, mesh=mesh, in_specs=in_specs, out_specs=out_specs, check_vma=False)
```

profile of v0, /device:TPU:0, one launch (start us, length us, event | category | flops | bytes accessed | tf_op | source)
XLA Modules:
  0.0 385.8 jit_solution(3843586543527307721)
XLA Ops:
  7.2 12.1 %all_to_all.134 = bf16[8,4,32]{2,1,0:T(4,128)(2,1)S(1)} all-to-all(bf16[8,4,32]{2,1,0:T(4,128)(2,1)} %bitcast.263), channel_id=1, replica_groups=mesh['rows'=4,'cols'=8] {'cols'}, dimensions={0} | all-to-all | bytes 4096 | tf_op jit(solution)/shard_map/all_to_all | solution.py:193
  19.3 3.6 all-to-all-start.1
  24.4 13.7 %all-to-all-done.1 = bf16[32,32,256]{2,1,0:T(8,128)(2,1)S(1)} async-done(((bf16[32,32,256]{2,1,0:T(8,128)(2,1)}), bf16[32,32,256]{2,1,0:T(8,128)(2,1)S(1)}, u32[]{:S(2)}, u32[]{:S(2)}) %all-to-all-start.1) | async-done | bytes 524320 | tf_op jit(solution)/shard_map/all_to_all | solution.py:192
  38.2 3.7 all-to-all-start.5
  46.3 4.7 %fusion.124 = (f32[4,4,256]{2,1,0:T(4,128)S(1)}, f32[4,4,256,256]{2,3,1,0:T(8,128)}) fusion(f32[4,256]{1,0:T(4,128)S(1)} %reshape.252, bf16[4,256,4,64]{1,3,2,0:T(8,128)(2,1)S(1)} %bitcast.249, bf16[4,256,4,64]{1,3,2,0:T(8,128)(2,1)} %bitcast.247), kind=kOutput, calls=%fused_computation.165 | convolution fusion | flops 138412288 | bytes 5263360 | tf_op jit(solution)/shard_map/while/body/eval_jaxpr/sub | solution.py:72
  51.0 2.7 convolution_convert_fusion.7
  54.9 1.2 copy.374
  56.1 3.5 all-to-all-start.3
  59.6 1.1 copy.364
  60.7 14.2 %all-to-all-done.3 = bf16[4,256,256]{2,0,1:T(4,128)(2,1)S(1)} async-done(((bf16[4,256,256]{2,0,1:T(4,128)(2,1)}), bf16[4,256,256]{2,0,1:T(4,128)(2,1)S(1)}, u32[]{:S(2)}, u32[]{:S(2)}) %all-to-all-start.3) | async-done | bytes 524320 | tf_op jit(solution)/shard_map/all_to_all | solution.py:199
  74.8 4.2 %all-to-all-start = ((bf16[32,32,256]{2,0,1:T(8,128)(2,1)}), bf16[32,32,256]{2,0,1:T(8,128)(2,1)S(1)}, u32[]{:S(2)}, u32[]{:S(2)}) async-start(bf16[32,32,256]{2,0,1:T(8,128)(2,1)} %copy.364), calls=%async_computation | async-start | bytes 1048576 | tf_op jit(solution)/shard_map/all_to_all | solution.py:206
  79.2 1.1 copy.377
  80.2 6.6 %all-to-all-done = bf16[32,32,256]{2,0,1:T(8,128)(2,1)S(1)} async-done(((bf16[32,32,256]{2,0,1:T(8,128)(2,1)}), bf16[32,32,256]{2,0,1:T(8,128)(2,1)S(1)}, u32[]{:S(2)}, u32[]{:S(2)}) %all-to-all-start) | async-done | bytes 524320 | tf_op jit(solution)/shard_map/all_to_all | solution.py:206
  86.9 3.7 all-to-all-start.4
  91.5 5.8 %all-to-all-done.4 = bf16[32,32,256]{2,0,1:T(8,128)(2,1)S(1)} async-done(((bf16[32,32,256]{2,0,1:T(8,128)(2,1)}), bf16[32,32,256]{2,0,1:T(8,128)(2,1)S(1)}, u32[]{:S(2)}, u32[]{:S(2)}) %all-to-all-start.4) | async-done | bytes 524320 | tf_op jit(solution)/shard_map/all_to_all | solution.py:198
  100.8 1.6 convolution_convert_fusion
  102.3 1.1 fusion.122
  103.5 2.0 copy.387
  106.5 1.3 copy.385
  107.9 3.7 fusion.125
  111.6 2.0 convolution_convert_fusion.6
  115.3 2.8 multiply_convert_fusion
  118.2 3.2 fusion.10
  122.3 1.0 fusion.69
  124.2 1.1 convolution_convert_fusion.3
  125.3 2.0 copy.392
  127.3 3.5 convolution_convert_fusion.5
  130.8 1.8 fusion.126
  132.6 5.2 %fusion.42 = bf16[8,4,64,128]{3,2,1,0:T(8,128)(2,1)} fusion(bf16[128,8,4,64]{0,3,2,1:T(8,128)(2,1)} %bitcast.252, f32[8,4,128,128]{2,3,1,0:T(8,128)} %fusion.126, f32[8,4,128,128]{2,3,1,0:T(8,128)} %get-tuple-element.127, f32[8,4,128]{2,1,0:T(4,128)S(1)} %get-tuple-element.126), kind=kOutput, calls=%fused_computation.49 | convolution fusion | flops 71045248 | bytes 5259264 | tf_op jit(solution)/shard_map/while/body/eval_jaxpr/shqk,kshd->qshd/dot_general | solution.py:10
  137.9 5.0 %fusion.45 = bf16[8,4,64,128]{3,2,1,0:T(8,128)(2,1)} fusion(bf16[128,8,4,64]{0,3,2,1:T(8,128)(2,1)S(1)} %bitcast.254, f32[8,4,128,128]{2,3,1,0:T(8,128)} %fusion.126, f32[8,4,128,128]{2,3,1,0:T(8,128)} %get-tuple-element.127, f32[8,4,128]{2,1,0:T(4,128)S(1)} %get-tuple-element.126), kind=kOutput, calls=%fused_computation.50 | convolution fusion | flops 71045248 | bytes 5259264 | tf_op jit(solution)/shard_map/while/body/eval_jaxpr/shqk,qshd->kshd/dot_general | solution.py:10
  142.9 1.2 copy.398
  144.1 2.2 copy.397
  146.4 2.0 copy.396
  148.4 3.2 multiply_reduce_fusion.2
  152.5 1.1 copy.399
  153.6 4.1 %all-to-all-start.6 = ((bf16[128,8,256]{2,1,0:T(8,128)(2,1)}), bf16[128,8,256]{2,1,0:T(8,128)(2,1)}, u32[]{:S(2)}, u32[]{:S(2)}) async-start(bf16[128,8,256]{2,1,0:T(8,128)(2,1)} %copy.399), calls=%async_computation.6 | async-start | bytes 1048576 | tf_op jit(solution)/shard_map/all_to_all | solution.py:221
  157.7 1.1 copy.420
  160.1 1.8 copy.416
  162.0 1.5 reshape_reshape.3
  164.3 1.9 copy.454
  166.3 3.5 all-to-all-start.7
  170.1 2.3 convolution_multiply_fusion
  172.3 3.0 fusion.56
  175.3 2.0 fusion.38
  177.3 2.4 fusion.39
  179.7 5.3 %all-to-all-done.7 = bf16[32,32,256]{2,1,0:T(8,128)(2,1)S(1)} async-done(((bf16[32,32,256]{2,1,0:T(8,128)(2,1)}), bf16[32,32,256]{2,1,0:T(8,128)(2,1)S(1)}, u32[]{:S(2)}, u32[]{:S(2)}) %all-to-all-start.7) | async-done | bytes 524320 | tf_op jit(solution)/shard_map/all_to_all | solution.py:220
  185.4 3.8 convolution_convert_fusion.4
  189.3 2.7 fusion.127
  192.0 8.0 %fusion.48 = bf16[4,4,64,256]{3,2,1,0:T(8,128)(2,1)} fusion(bf16[4,256,4,64]{1,3,2,0:T(8,128)(2,1)S(1)} %bitcast.248, f32[4,4,256,256]{2,3,1,0:T(8,128)} %fusion.127, f32[4,4,256,256]{2,3,1,0:T(8,128)} %get-tuple-element.125, f32[4,4,256]{2,1,0:T(4,128)S(1)} %get-tuple-element.124), kind=kOutput, calls=%fused_computation.51 | convolution fusion | flops 141824256 | bytes 9453568 | tf_op jit(solution)/shard_map/while/body/eval_jaxpr/shqk,skhd->sqhd/dot_general | solution.py:10
  200.0 8.0 %fusion.51 = bf16[4,4,64,256]{3,2,1,0:T(8,128)(2,1)} fusion(bf16[4,256,4,64]{1,3,2,0:T(8,128)(2,1)S(1)} %bitcast.250, f32[4,4,256,256]{2,3,1,0:T(8,128)} %fusion.127, f32[4,4,256,256]{2,3,1,0:T(8,128)} %get-tuple-element.125, f32[4,4,256]{2,1,0:T(4,128)S(1)} %get-tuple-element.124), kind=kOutput, calls=%fused_computation.52 | convolution fusion | flops 141824256 | bytes 9453568 | tf_op jit(solution)/shard_map/while/body/eval_jaxpr/shqk,sqhd->skhd/dot_general | solution.py:10
  208.0 1.3 copy.407
  209.3 2.1 copy.406
  211.4 2.0 copy.405
  213.5 1.0 convolution_multiply_fusion.1
  214.5 2.7 fusion.57
  217.2 1.0 copy-done.34
  218.5 1.3 multiply_reduce_fusion.3
  220.7 1.2 copy.409
  221.9 3.5 all-to-all-start.8
  225.4 41.2 %all-reduce = (f32[256]{0:T(256)}, f32[256]{0:T(256)}, f32[256]{0:T(256)}) all-reduce(f32[256]{0:T(256)S(1)} %broadcast_multiply_fusion.11, f32[256]{0:T(256)S(1)} %broadcast_multiply_fusion.10, f32[256]{0:T(256)S(1)} %broadcast_multiply_fusion.9), channel_id=1, replica_groups=mesh['rows'=4,'cols'=8] {'rows','cols'}, use_global_device_ids=true, to_apply=%region_19.20 | all-reduce | flops 768 | bytes 6144 | tf_op jit(solution)/shard_map/psum | solution.py:232
  267.6 102.7 %all-reduce.4.cloned.1.call-done = (f32[256,768]{1,0:T(8,128)}, f32[256,256]{1,0:T(8,128)}, f32[256,768]{1,0:T(8,128)}, f32[256,256]{1,0:T(8,128)}, f32[256,1024]{1,0:T(8,128)}, /*index=5*/f32[1024,256]{1,0:T(8,128)}) async-done(((f32[256,768]{1,0:T(8,128)}, f32[256,256]{1,0:T(8,128)}, f32[256,768]{1,0:T(8,128)}, f32[256,256]{1,0:T(8,128)}, f32[256,1024]{1,0:T(8,128)}, /*index=5*/f32[1024,256]{1,0:T(8,128)}), ...) | async-done | bytes 4194320 | tf_op jit(solution)/shard_map/psum | solution.py:232
  370.2 2.2 copy.461
  372.5 1.7 copy.462
  374.2 2.1 copy.463
  (162 shorter events, 24.5 us)
Async XLA Ops:
  7.2 108.1 %copy-start = (bf16[256,1024]{1,0:T(8,128)(2,1)S(1)}, bf16[256,1024]{1,0:T(8,128)(2,1)}, u32[]{:S(2)}) copy-start(bf16[256,1024]{1,0:T(8,128)(2,1)} %param.22) | copy-start | bytes 1572868
  19.3 23.7 %copy-start.41 = (f32[256]{0:T(256)S(1)}, f32[256]{0:T(256)}, u32[]{:S(2)}) copy-start(f32[256]{0:T(256)} %param.15) | copy-start | bytes 3076
  19.3 18.9 %all-to-all-start.1 = ((bf16[32,32,256]{2,1,0:T(8,128)(2,1)}), bf16[32,32,256]{2,1,0:T(8,128)(2,1)S(1)}, u32[]{:S(2)}, u32[]{:S(2)}) async-start(bf16[32,32,256]{2,1,0:T(8,128)(2,1)} %param.12), calls=%async_computation.1 | async-start | bytes 1048576 | tf_op jit(solution)/shard_map/all_to_all | solution.py:192
  38.2 17.9 %all-to-all-start.5 = ((bf16[4,2,128]{2,1,0:T(2,128)(2,1)}), bf16[4,2,128]{2,1,0:T(2,128)(2,1)S(1)}, u32[]{:S(2)}, u32[]{:S(2)}) async-start(bf16[4,2,128]{2,1,0:T(2,128)(2,1)} %reshape.268), calls=%async_computation.5 | async-start | bytes 4096 | tf_op jit(solution)/shard_map/all_to_all | solution.py:207
  41.9 2.2 copy-start.36
  43.3 0.8 copy-start.15
  46.0 4.9 %copy-start.29 = (bf16[4,256,256]{1,2,0:T(8,128)(2,1)}, bf16[4,256,256]{1,2,0:T(8,128)(2,1)S(1)}, u32[]{:S(2)}) copy-start(bf16[4,256,256]{1,2,0:T(8,128)(2,1)S(1)} %copy.369) | copy-start | bytes 1572868
  46.2 4.7 %copy-start.8 = (bf16[4,256,256]{1,2,0:T(8,128)(2,1)}, bf16[4,256,256]{1,2,0:T(8,128)(2,1)S(1)}, u32[]{:S(2)}) copy-start(bf16[4,256,256]{1,2,0:T(8,128)(2,1)S(1)} %copy.368) | copy-start | bytes 1572868
  50.9 3.6 copy-start.26
  53.7 0.8 copy-start.10
  53.7 5.9 %copy-start.27 = (bf16[32,32,256]{2,1,0:T(8,128)(2,1)S(1)}, bf16[32,32,256]{2,1,0:T(8,128)(2,1)}, u32[]{:S(2)}) copy-start(bf16[32,32,256]{2,1,0:T(8,128)(2,1)} %param.14) | copy-start | bytes 1572868
  56.1 18.8 %all-to-all-start.3 = ((bf16[4,256,256]{2,0,1:T(4,128)(2,1)}), bf16[4,256,256]{2,0,1:T(4,128)(2,1)S(1)}, u32[]{:S(2)}, u32[]{:S(2)}) async-start(bf16[4,256,256]{2,0,1:T(4,128)(2,1)} %copy.374), calls=%async_computation.3 | async-start | bytes 1048576 | tf_op jit(solution)/shard_map/all_to_all | solution.py:199
  74.8 12.0 %all-to-all-start = ((bf16[32,32,256]{2,0,1:T(8,128)(2,1)}), bf16[32,32,256]{2,0,1:T(8,128)(2,1)S(1)}, u32[]{:S(2)}, u32[]{:S(2)}) async-start(bf16[32,32,256]{2,0,1:T(8,128)(2,1)} %copy.364), calls=%async_computation | async-start | bytes 1048576 | tf_op jit(solution)/shard_map/all_to_all | solution.py:206
  86.9 11.8 %copy-start.2 = (bf16[32,32,256]{2,0,1:T(8,128)(2,1)}, bf16[32,32,256]{2,0,1:T(8,128)(2,1)S(1)}, u32[]{:S(2)}) copy-start(bf16[32,32,256]{2,0,1:T(8,128)(2,1)S(1)} %all-to-all-done) | copy-start | bytes 1572868
  86.9 10.4 %all-to-all-start.4 = ((bf16[32,32,256]{2,0,1:T(8,128)(2,1)}), bf16[32,32,256]{2,0,1:T(8,128)(2,1)S(1)}, u32[]{:S(2)}, u32[]{:S(2)}) async-start(bf16[32,32,256]{2,0,1:T(8,128)(2,1)} %copy.377), calls=%async_computation.4 | async-start | bytes 1048576 | tf_op jit(solution)/shard_map/all_to_all | solution.py:198
  90.7 8.9 %copy-start.40 = (f32[256]{0:T(256)S(1)}, f32[256]{0:T(256)}, u32[]{:S(2)}) copy-start(f32[256]{0:T(256)} %param.18) | copy-start | bytes 3076
  100.0 0.8 copy-start.17
  107.9 5.8 %copy-start.20 = (bf16[128,8,256]{0,2,1:T(8,128)(2,1)}, bf16[128,8,256]{0,2,1:T(8,128)(2,1)S(1)}, u32[]{:S(2)}) copy-start(bf16[128,8,256]{0,2,1:T(8,128)(2,1)S(1)} %copy.385) | copy-start | bytes 1572868
  111.6 2.9 copy-start.25
  111.6 3.8 copy-start.39
  113.6 0.8 copy-start.7
  115.3 2.8 copy-start.12
  115.3 2.8 copy-start.44
  121.4 2.0 copy-start.13
  123.4 0.8 copy-start.4
  127.3 3.5 copy-start.21
  127.3 3.5 copy-start.22
  132.6 5.2 %copy-start.32 = (bf16[128,8,256]{0,2,1:T(8,128)(2,1)S(1)}, bf16[128,8,256]{0,2,1:T(8,128)(2,1)}, u32[]{:S(2)}) copy-start(bf16[128,8,256]{0,2,1:T(8,128)(2,1)} %copy.386) | copy-start | bytes 1572868
  144.1 4.3 %copy-start.31 = (bf16[128,8,256]{2,0,1:T(8,128)(2,1)}, bf16[128,8,256]{2,0,1:T(8,128)(2,1)S(1)}, u32[]{:S(2)}) copy-start(bf16[128,8,256]{2,0,1:T(8,128)(2,1)S(1)} %copy.398) | copy-start | bytes 1572868
  148.4 3.2 copy-start.5
  151.6 6.1 %copy-start.3 = (bf16[32,32,256]{2,0,1:T(8,128)(2,1)S(1)}, bf16[32,32,256]{2,0,1:T(8,128)(2,1)}, u32[]{:S(2)}) copy-start(bf16[32,32,256]{2,0,1:T(8,128)(2,1)} %copy-done.2) | copy-start | bytes 1572868
  152.5 6.3 %copy-start.11 = (bf16[4,4,64,256]{3,2,1,0:T(8,128)(2,1)S(1)}, bf16[4,4,64,256]{3,2,1,0:T(8,128)(2,1)}, u32[]{:S(2)}) copy-start(bf16[4,4,64,256]{3,2,1,0:T(8,128)(2,1)} %copy-done.10) | copy-start | bytes 1572868
  153.6 10.8 %all-to-all-start.6 = ((bf16[128,8,256]{2,1,0:T(8,128)(2,1)}), bf16[128,8,256]{2,1,0:T(8,128)(2,1)}, u32[]{:S(2)}, u32[]{:S(2)}) async-start(bf16[128,8,256]{2,1,0:T(8,128)(2,1)} %copy.399), calls=%async_computation.6 | async-start | bytes 1048576 | tf_op jit(solution)/shard_map/all_to_all | solution.py:221
  159.2 10.9 %copy-start.6 = (bf16[128,8,256]{2,0,1:T(8,128)(2,1)S(1)}, bf16[128,8,256]{2,0,1:T(8,128)(2,1)}, u32[]{:S(2)}) copy-start(bf16[128,8,256]{2,0,1:T(8,128)(2,1)} %copy-done.4) | copy-start | bytes 1572868
  163.5 8.9 %copy-start.18 = (bf16[128,8,256]{2,0,1:T(8,128)(2,1)S(1)}, bf16[128,8,256]{2,0,1:T(8,128)(2,1)}, u32[]{:S(2)}) copy-start(bf16[128,8,256]{2,0,1:T(8,128)(2,1)} %copy-done.17) | copy-start | bytes 1572868
  166.3 18.8 %all-to-all-start.7 = ((bf16[32,32,256]{2,1,0:T(8,128)(2,1)}), bf16[32,32,256]{2,1,0:T(8,128)(2,1)S(1)}, u32[]{:S(2)}, u32[]{:S(2)}) async-start(bf16[32,32,256]{2,1,0:T(8,128)(2,1)} %bitcast.239), calls=%async_computation.7 | async-start | bytes 1048576 | tf_op jit(solution)/shard_map/all_to_all | solution.py:220
  169.8 200.5 %all-reduce.4.cloned.1.call-start = ((), (), s32[]{:S(2)}) async-start(), calls=%async_computation.9 | async-start | bytes 8388608 | tf_op jit(solution)/shard_map/psum | solution.py:232
  172.3 3.0 copy-start.14
  175.3 2.0 copy-start.33
  175.3 2.0 copy-start.45
  185.4 3.8 copy-start.9
  189.3 2.7 copy-start.28
  192.0 8.0 %copy-start.30 = (bf16[4,256,256]{1,2,0:T(8,128)(2,1)S(1)}, bf16[4,256,256]{1,2,0:T(8,128)(2,1)}, u32[]{:S(2)}) copy-start(bf16[4,256,256]{1,2,0:T(8,128)(2,1)} %copy-done.29) | copy-start | bytes 1572868
  208.0 5.5 %copy-start.19 = (bf16[32,8,4,256]{3,1,2,0:T(8,128)(2,1)S(1)}, bf16[32,8,4,256]{3,1,2,0:T(8,128)(2,1)}, u32[]{:S(2)}) copy-start(bf16[32,8,4,256]{3,1,2,0:T(8,128)(2,1)} %copy.437) | copy-start | bytes 1572868
  208.0 6.5 %copy-start.16 = (bf16[4,256,256]{2,1,0:T(8,128)(2,1)S(1)}, bf16[4,256,256]{2,1,0:T(8,128)(2,1)}, u32[]{:S(2)}) copy-start(bf16[4,256,256]{2,1,0:T(8,128)(2,1)} %copy-done.15) | copy-start | bytes 1572868
  217.2 1.0 copy-start.34
  217.2 1.2 copy-start.35
  217.2 1.3 copy-start.37
  219.8 5.6 %copy-start.42 = (f32[256]{0:T(256)S(1)}, f32[256]{0:T(256)}, u32[]{:S(2)}) copy-start(f32[256]{0:T(256)} %get-tuple-element.73) | copy-start | bytes 3076
  219.8 5.6 %copy-start.43 = (f32[256]{0:T(256)S(1)}, f32[256]{0:T(256)}, u32[]{:S(2)}) copy-start(f32[256]{0:T(256)} %get-tuple-element.84) | copy-start | bytes 3076
  221.9 44.8 %all-to-all-start.8 = ((bf16[4,256,256]{2,0,1:T(4,128)(2,1)}), bf16[4,256,256]{2,0,1:T(4,128)(2,1)S(1)}, u32[]{:S(2)}, u32[]{:S(2)}) async-start(bf16[4,256,256]{2,0,1:T(4,128)(2,1)} %copy.409), calls=%async_computation.8 | async-start | bytes 1048576 | tf_op jit(solution)/shard_map/all_to_all | solution.py:230
  370.2 6.0 %copy-start.38 = (f32[256,256]{1,0:T(8,128)S(1)}, f32[256,256]{1,0:T(8,128)}, u32[]{:S(2)}) copy-start(f32[256,256]{1,0:T(8,128)} %get-tuple-element.143) | copy-start | bytes 786436
  370.2 6.7 %copy-start.24 = (f32[256,1024]{1,0:T(8,128)S(1)}, f32[256,1024]{1,0:T(8,128)}, u32[]{:S(2)}) copy-start(f32[256,1024]{1,0:T(8,128)} %get-tuple-element.145) | copy-start | bytes 3145732
  370.2 7.7 %copy-start.23 = (f32[1024,256]{1,0:T(8,128)S(1)}, f32[1024,256]{1,0:T(8,128)}, u32[]{:S(2)}) copy-start(f32[1024,256]{1,0:T(8,128)} %get-tuple-element.146) | copy-start | bytes 3145732
  372.5 6.4 %copy-start.1 = (bf16[256,1024]{1,0:T(8,128)(2,1)S(1)}, bf16[256,1024]{1,0:T(8,128)(2,1)}, u32[]{:S(2)}) copy-start(bf16[256,1024]{1,0:T(8,128)(2,1)} %param.22) | copy-start | bytes 1572868
Sparse Core Ops, SparseCore 0:
  217.3 152.8 all-reduce.3
where the time goes:
time: 387 us; the launch traced here: 386 us
  waiting for transfers between devices  149 us (39%)
  matrix products  80.4 us (21%)
  blocking collectives  53.3 us (14%)
  local copies, waits for them, and re-layouts  52.3 us (14%)
  starting transfers between devices  30.1 us (8%)
  between operations  14.7 us (4%)
  other arithmetic  5.81 us (2%)
    psum x1, waiting for transfers between devices, shards(): lax.psum((row_sums[0], row_sums[1], row_sums[2], other_sums[0], other_sum...  103 us
    dot_general x10, matrix products, product(): jnp.einsum(spec_text, left_op, right_op, preferred_element_type=jnp.float32)  42.8 us
    psum x1, blocking collectives, shards(): lax.psum((row_sums[0], row_sums[1], row_sums[2], other_sums[0], other_sum...  41.2 us
    unnamed x104, local copies, waits for them, and re-layouts  17.6 us
    all_to_all x1, waiting for transfers between devices, shards(): lax.all_to_all(after_rows, 'cols', split_axis=1, concat_axis=0, tiled=True)  14.2 us
    all_to_all x1, waiting for transfers between devices, shards(): lax.all_to_all(tokens, 'cols', split_axis=0, concat_axis=1, tiled=True)  13.7 us
    dot_general x6, matrix products, over_cells(): lax.dot_general(left_flat, right_flat, (((0,), (0,)), ((), ())), preferre...  13.3 us
    all_to_all x1, blocking collectives, shards(): lax.all_to_all(key_bias, 'cols', split_axis=0, concat_axis=1, tiled=True)  12.1 us
  transfers between devices with their start and end apart: 9, of which 7 were waited for; matrix products, arithmetic and copies ran while one was open for 10% of the time, Pallas kernels for 0%

commit v1 on v0

--- a/solution.py
+++ b/solution.py
@@ -1,9 +1,42 @@
+import functools
 import jax
 import jax.numpy as jnp
 from jax import lax
 from jax.sharding import PartitionSpec as P
 
 HEADS = 4
+
+
+def handle_shapes(point, out_dim, block_here):
+    aux = point.shape
+    local_next = point.reshape(
+        *aux[:out_dim], block_here, aux[out_dim] // block_here, *aux[out_dim + 1 :]
+    )
+    return jnp.moveaxis(local_next, out_dim, 0)
+
+
+def mark_vector(page, d_out):
+    page = jnp.moveaxis(page, 0, d_out)
+    reached = page.shape
+    return page.reshape(
+        *reached[:d_out], reached[d_out] * reached[d_out + 1], *reached[d_out + 2 :]
+    )
+
+
+def _pair_sections(xin, lane_axis, shard_in, my_data):
+    all_values = lax.psum(1, lane_axis)
+    field_out, back = (all_values, lax.axis_index(lane_axis))
+    o_now = handle_shapes(xin, shard_in, field_out)
+    trail = [o_now[back]]
+    for dev_j in tuple(range(1, field_out)):
+        y = o_now[back ^ dev_j]
+        next_value = lax.ppermute(y, lane_axis, [(k, k ^ dev_j) for k in range(field_out)])
+        trail.append(next_value)
+    o_now = jnp.stack(trail, axis=0)[back ^ jnp.arange(field_out)]
+    return mark_vector(o_now, my_data)
+
+
+report_array = functools.partial(_pair_sections, lane_axis="rows", shard_in=1, my_data=0)
 
 
 def product(spec_text, left_op, right_op):
@@ -203,7 +236,7 @@
         tiled=True,
     )
     column_grads, column_bias = (
-        lax.all_to_all(cotangent, "rows", split_axis=1, concat_axis=0, tiled=True),
+        report_array(cotangent),
         lax.all_to_all(key_bias, "rows", split_axis=1, concat_axis=0, tiled=True),
     )
     after_cols, column_saved = attention_forward(

time: 387 us -> 380 us (0.982)
  waiting for transfers between devices: 149 us -> 143 us
    all_to_all x1 -> x0, waiting for transfers between devices: 6.62 us -> none  [shards(): lax.all_to_all(cotangent, 'rows', split_axis=1, concat_axis=0, tiled=True)]
    all_to_all x1 -> x0, starting transfers between devices: 4.19 us -> none  [shards(): lax.all_to_all(cotangent, 'rows', split_axis=1, concat_axis=0, tiled=True)]
    unnamed x104 -> x91, local copies, waits for them, and re-layouts: 17.6 us -> 15 us
  transfers between devices with their start and end apart: 9 -> 11, of which waited for: 7 -> 7; matrix products, arithmetic and copies ran while one was open for 10% -> 6% of each run, Pallas kernels for 0% -> 0%
where the time goes in v1:
time: 380 us; the launch traced here: 378 us
  waiting for transfers between devices  143 us (38%)
  matrix products  80.7 us (21%)
  blocking collectives  53.2 us (14%)
  local copies, waits for them, and re-layouts  51.1 us (13%)
  starting transfers between devices  29.5 us (8%)
  between operations  14.7 us (4%)
  other arithmetic  5.88 us (2%)
    psum x1, waiting for transfers between devices, shards(): lax.psum((row_sums[0], row_sums[1], row_sums[2], other_sums[0], other_sum...  103 us
    dot_general x10, matrix products, product(): jnp.einsum(spec_text, left_op, right_op, preferred_element_type=jnp.float32)  43.1 us
    psum x1, blocking collectives, shards(): lax.psum((row_sums[0], row_sums[1], row_sums[2], other_sums[0], other_sum...  41.2 us
    all_to_all x1, waiting for transfers between devices, shards(): lax.all_to_all(tokens, 'cols', split_axis=0, concat_axis=1, tiled=True)  15.2 us
    unnamed x91, local copies, waits for them, and re-layouts  15 us
    dot_general x6, matrix products, over_cells(): lax.dot_general(left_flat, right_flat, (((0,), (0,)), ((), ())), preferre...  13.3 us
    all_to_all x1, blocking collectives, shards(): lax.all_to_all(key_bias, 'cols', split_axis=0, concat_axis=1, tiled=True)  12.1 us
    all_to_all x1, waiting for transfers between devices, shards(): lax.all_to_all(after_rows, 'cols', split_axis=1, concat_axis=0, tiled=True)  10.8 us
  transfers between devices with their start and end apart: 11, of which 7 were waited for; matrix products, arithmetic and copies ran while one was open for 6% of the time, Pallas kernels for 0%

profile of v1, /device:TPU:0, one launch (start us, length us, event | category | flops | bytes accessed | tf_op | source)
XLA Modules:
  0.0 378.1 jit_solution(9285951788832923822)
XLA Ops:
  7.2 12.1 %all_to_all.116 = bf16[8,4,32]{2,1,0:T(4,128)(2,1)S(1)} all-to-all(bf16[8,4,32]{2,1,0:T(4,128)(2,1)} %bitcast.282), channel_id=1, replica_groups=mesh['rows'=4,'cols'=8] {'cols'}, dimensions={0} | all-to-all | bytes 4096 | tf_op jit(solution)/shard_map/all_to_all | solution.py:226
  19.3 3.6 all-to-all-start
  23.0 15.2 %all-to-all-done = bf16[32,32,256]{2,1,0:T(8,128)(2,1)S(1)} async-done(((bf16[32,32,256]{2,1,0:T(8,128)(2,1)}), bf16[32,32,256]{2,1,0:T(8,128)(2,1)S(1)}, u32[]{:S(2)}, u32[]{:S(2)}) %all-to-all-start) | async-done | bytes 524320 | tf_op jit(solution)/shard_map/all_to_all | solution.py:225
  42.5 4.7 %fusion.125 = (f32[4,4,256]{2,1,0:T(4,128)S(1)}, f32[4,4,256,256]{2,3,1,0:T(8,128)}) fusion(f32[4,256]{1,0:T(4,128)S(1)} %reshape.278, bf16[4,256,4,64]{1,3,2,0:T(8,128)(2,1)S(1)} %bitcast.266, bf16[4,256,4,64]{1,3,2,0:T(8,128)(2,1)} %bitcast.264), kind=kOutput, calls=%fused_computation.174 | convolution fusion | flops 138412288 | bytes 5263360 | tf_op jit(solution)/shard_map/while/body/eval_jaxpr/sub | solution.py:105
  47.2 2.7 convolution_convert_fusion.7
  51.1 1.2 copy.386
  52.3 3.5 all-to-all-start.2
  56.0 1.6 collective-permute-start.1
  57.6 1.5 collective-permute-start
  60.3 10.8 %all-to-all-done.2 = bf16[4,256,256]{2,0,1:T(4,128)(2,1)S(1)} async-done(((bf16[4,256,256]{2,0,1:T(4,128)(2,1)}), bf16[4,256,256]{2,0,1:T(4,128)(2,1)S(1)}, u32[]{:S(2)}, u32[]{:S(2)}) %all-to-all-start.2) | async-done | bytes 524320 | tf_op jit(solution)/shard_map/all_to_all | solution.py:232
  71.1 3.7 all-to-all-start.4
  75.0 1.1 copy.389
  76.0 3.4 all-to-all-done.4
  79.4 3.7 all-to-all-start.3
  84.9 4.7 %all-to-all-done.3 = bf16[32,32,256]{2,0,1:T(8,128)(2,1)S(1)} async-done(((bf16[32,32,256]{2,0,1:T(8,128)(2,1)}), bf16[32,32,256]{2,0,1:T(8,128)(2,1)S(1)}, u32[]{:S(2)}, u32[]{:S(2)}) %all-to-all-start.3) | async-done | bytes 524320 | tf_op jit(solution)/shard_map/all_to_all | solution.py:231
  93.1 1.6 convolution_convert_fusion
  94.7 1.1 fusion.123
  95.8 2.0 copy.399
  98.8 1.3 copy.397
  100.2 3.7 fusion.126
  103.9 2.0 convolution_convert_fusion.6
  107.7 2.9 multiply_convert_fusion
  110.5 3.2 fusion.10
  114.7 1.0 fusion.69
  115.7 1.1 convolution_convert_fusion.3
  116.8 2.0 copy.404
  118.9 3.5 convolution_convert_fusion.5
  122.4 1.8 fusion.127
  124.2 5.2 %fusion.42 = bf16[8,4,64,128]{3,2,1,0:T(8,128)(2,1)} fusion(bf16[128,8,4,64]{0,3,2,1:T(8,128)(2,1)} %bitcast.269, f32[8,4,128,128]{2,3,1,0:T(8,128)} %fusion.127, f32[8,4,128,128]{2,3,1,0:T(8,128)} %get-tuple-element.131, f32[8,4,128]{2,1,0:T(4,128)S(1)} %get-tuple-element.130), kind=kOutput, calls=%fused_computation.50 | convolution fusion | flops 71045248 | bytes 5259264 | tf_op jit(solution)/shard_map/while/body/eval_jaxpr/shqk,kshd->qshd/dot_general | solution.py:43
  129.4 5.2 %fusion.45 = bf16[8,4,64,128]{3,2,1,0:T(8,128)(2,1)} fusion(bf16[128,8,4,64]{0,3,2,1:T(8,128)(2,1)} %bitcast.271, f32[8,4,128,128]{2,3,1,0:T(8,128)} %fusion.127, f32[8,4,128,128]{2,3,1,0:T(8,128)} %get-tuple-element.131, f32[8,4,128]{2,1,0:T(4,128)S(1)} %get-tuple-element.130), kind=kOutput, calls=%fused_computation.51 | convolution fusion | flops 71045248 | bytes 5259264 | tf_op jit(solution)/shard_map/while/body/eval_jaxpr/shqk,qshd->kshd/dot_general | solution.py:43
  134.6 2.0 copy.410
  136.7 2.0 copy.409
  138.7 2.0 copy.408
  140.8 3.2 multiply_reduce_fusion.2
  144.8 1.1 copy.411
  145.9 4.1 %all-to-all-start.5 = ((bf16[128,8,256]{2,1,0:T(8,128)(2,1)}), bf16[128,8,256]{2,1,0:T(8,128)(2,1)}, u32[]{:S(2)}, u32[]{:S(2)}) async-start(bf16[128,8,256]{2,1,0:T(8,128)(2,1)} %copy.411), calls=%async_computation.5 | async-start | bytes 1048576 | tf_op jit(solution)/shard_map/all_to_all | solution.py:254
  150.0 1.5 copy.425
  152.4 1.8 copy.428
  154.3 1.5 reshape_reshape.6
  156.7 2.0 copy.467
  158.6 3.5 all-to-all-start.6
  162.5 2.3 convolution_multiply_fusion
  164.7 3.0 fusion.56
  167.7 2.0 fusion.38
  169.7 2.4 fusion.39
  172.1 5.3 %all-to-all-done.6 = bf16[32,32,256]{2,1,0:T(8,128)(2,1)S(1)} async-done(((bf16[32,32,256]{2,1,0:T(8,128)(2,1)}), bf16[32,32,256]{2,1,0:T(8,128)(2,1)S(1)}, u32[]{:S(2)}, u32[]{:S(2)}) %all-to-all-start.6) | async-done | bytes 524320 | tf_op jit(solution)/shard_map/all_to_all | solution.py:253
  177.8 3.8 %convolution_convert_fusion.4 = bf16[4,4,64,256]{3,2,1,0:T(8,128)(2,1)} fusion(bf16[4,256,4,64]{1,3,2,0:T(8,128)(2,1)S(1)} %bitcast.249, f32[4,4,256,256]{2,3,1,0:T(8,128)} %get-tuple-element.129, f32[4,4,256]{2,1,0:T(4,128)S(1)} %get-tuple-element.128), kind=kOutput, calls=%fused_computation.56 | convolution fusion | flops 136577024 | bytes 5259264 | tf_op jit(solution)/shard_map/while/body/eval_jaxpr/shqk,sqhd->skhd/dot_general | solution.py:43
  181.6 2.7 fusion.128
  184.4 8.0 %fusion.48 = bf16[4,4,64,256]{3,2,1,0:T(8,128)(2,1)} fusion(bf16[4,256,4,64]{1,3,2,0:T(8,128)(2,1)S(1)} %bitcast.265, f32[4,4,256,256]{2,3,1,0:T(8,128)} %fusion.128, f32[4,4,256,256]{2,3,1,0:T(8,128)} %get-tuple-element.129, f32[4,4,256]{2,1,0:T(4,128)S(1)} %get-tuple-element.128), kind=kOutput, calls=%fused_computation.52 | convolution fusion | flops 141824256 | bytes 9453568 | tf_op jit(solution)/shard_map/while/body/eval_jaxpr/shqk,skhd->sqhd/dot_general | solution.py:43
  192.4 8.0 %fusion.51 = bf16[4,4,64,256]{3,2,1,0:T(8,128)(2,1)} fusion(bf16[4,256,4,64]{1,3,2,0:T(8,128)(2,1)S(1)} %bitcast.267, f32[4,4,256,256]{2,3,1,0:T(8,128)} %fusion.128, f32[4,4,256,256]{2,3,1,0:T(8,128)} %get-tuple-element.129, f32[4,4,256]{2,1,0:T(4,128)S(1)} %get-tuple-element.128), kind=kOutput, calls=%fused_computation.53 | convolution fusion | flops 141824256 | bytes 9453568 | tf_op jit(solution)/shard_map/while/body/eval_jaxpr/shqk,sqhd->skhd/dot_general | solution.py:43
  200.4 1.3 copy.419
  201.7 2.1 copy.418
  203.9 2.0 copy.417
  205.9 1.0 convolution_multiply_fusion.1
  206.9 2.7 fusion.57
  209.6 1.0 copy-done.27
  210.9 1.3 multiply_reduce_fusion.3
  213.1 1.2 copy.421
  214.3 3.5 all-to-all-start.7
  217.9 41.2 %all-reduce = (f32[256]{0:T(256)}, f32[256]{0:T(256)}, f32[256]{0:T(256)}) all-reduce(f32[256]{0:T(256)S(1)} %broadcast_multiply_fusion.11, f32[256]{0:T(256)S(1)} %broadcast_multiply_fusion.10, f32[256]{0:T(256)S(1)} %broadcast_multiply_fusion.9), channel_id=1, replica_groups=mesh['rows'=4,'cols'=8] {'rows','cols'}, use_global_device_ids=true, to_apply=%region_19.20 | all-reduce | flops 768 | bytes 6144 | tf_op jit(solution)/shard_map/psum | solution.py:265
  259.9 102.7 %all-reduce.4.cloned.1.call-done = (f32[256,768]{1,0:T(8,128)}, f32[256,256]{1,0:T(8,128)}, f32[256,768]{1,0:T(8,128)}, f32[256,256]{1,0:T(8,128)}, f32[256,1024]{1,0:T(8,128)}, /*index=5*/f32[1024,256]{1,0:T(8,128)}) async-done(((f32[256,768]{1,0:T(8,128)}, f32[256,256]{1,0:T(8,128)}, f32[256,768]{1,0:T(8,128)}, f32[256,256]{1,0:T(8,128)}, f32[256,1024]{1,0:T(8,128)}, /*index=5*/f32[1024,256]{1,0:T(8,128)}), ...) | async-done | bytes 4194320 | tf_op jit(solution)/shard_map/psum | solution.py:265
  362.6 2.2 copy.474
  364.8 1.7 copy.475
  366.6 2.1 copy.476
  (157 shorter events, 23.9 us)
Async XLA Ops:
  7.2 100.4 %copy-start = (bf16[256,1024]{1,0:T(8,128)(2,1)S(1)}, bf16[256,1024]{1,0:T(8,128)(2,1)}, u32[]{:S(2)}) copy-start(bf16[256,1024]{1,0:T(8,128)(2,1)} %param.22) | copy-start | bytes 1572868
  19.3 19.9 %copy-start.35 = (f32[256]{0:T(256)S(1)}, f32[256]{0:T(256)}, u32[]{:S(2)}) copy-start(f32[256]{0:T(256)} %param.15) | copy-start | bytes 3076
  19.3 18.9 %all-to-all-start = ((bf16[32,32,256]{2,1,0:T(8,128)(2,1)}), bf16[32,32,256]{2,1,0:T(8,128)(2,1)S(1)}, u32[]{:S(2)}, u32[]{:S(2)}) async-start(bf16[32,32,256]{2,1,0:T(8,128)(2,1)} %param.12), calls=%async_computation | async-start | bytes 1048576 | tf_op jit(solution)/shard_map/all_to_all | solution.py:225
  23.0 17.4 %copy-start.29 = (bf16[256,768]{1,0:T(8,128)(2,1)S(1)}, bf16[256,768]{1,0:T(8,128)(2,1)}, u32[]{:S(2)}) copy-start(bf16[256,768]{1,0:T(8,128)(2,1)} %param.16) | copy-start | bytes 1179652
  39.6 0.8 copy-start.9
  42.3 4.9 %copy-start.25 = (bf16[4,256,256]{1,2,0:T(8,128)(2,1)}, bf16[4,256,256]{1,2,0:T(8,128)(2,1)S(1)}, u32[]{:S(2)}) copy-start(bf16[4,256,256]{1,2,0:T(8,128)(2,1)S(1)} %copy.381) | copy-start | bytes 1572868
  42.5 4.7 %copy-start.3 = (bf16[4,256,256]{1,2,0:T(8,128)(2,1)}, bf16[4,256,256]{1,2,0:T(8,128)(2,1)S(1)}, u32[]{:S(2)}) copy-start(bf16[4,256,256]{1,2,0:T(8,128)(2,1)S(1)} %copy.380) | copy-start | bytes 1572868
  47.2 3.5 copy-start.22
  50.0 0.8 copy-start.5
  50.0 5.9 %copy-start.23 = (bf16[32,32,256]{2,1,0:T(8,128)(2,1)S(1)}, bf16[32,32,256]{2,1,0:T(8,128)(2,1)}, u32[]{:S(2)}) copy-start(bf16[32,32,256]{2,1,0:T(8,128)(2,1)} %param.14) | copy-start | bytes 1572868
  50.0 9.6 %copy-start.32 = (bf16[32,32]{1,0:T(8,128)(2,1)S(1)}, bf16[32,32]{1,0:T(8,128)(2,1)}, u32[]{:S(2)}) copy-start(bf16[32,32]{1,0:T(8,128)(2,1)} %param.13) | copy-start | bytes 6148
  52.3 18.8 %all-to-all-start.2 = ((bf16[4,256,256]{2,0,1:T(4,128)(2,1)}), bf16[4,256,256]{2,0,1:T(4,128)(2,1)S(1)}, u32[]{:S(2)}, u32[]{:S(2)}) async-start(bf16[4,256,256]{2,0,1:T(4,128)(2,1)} %copy.386), calls=%async_computation.2 | async-start | bytes 1048576 | tf_op jit(solution)/shard_map/all_to_all | solution.py:232
  56.0 27.3 %collective-permute-start.1 = (bf16[32,8,256]{2,1,0:T(8,128)(2,1)S(1)}, bf16[32,8,256]{2,1,0:T(8,128)(2,1)S(1)}, u32[]{:S(2)}, u32[]{:S(2)}) collective-permute-start(bf16[32,8,256]{2,1,0:T(8,128)(2,1)S(1)} %get-tuple-element.125), channel_id=1, source_target_pairs={{0,16},{8,24},{16,0},{24,8},{1,17},{9,25},{17,1},{25,9},{2,18},{10... | collective-permute-start | bytes 393224 | tf_op jit(solution)/shard_map/ppermute | solution.py:33
  57.6 25.7 %collective-permute-start = (bf16[32,8,256]{2,1,0:T(8,128)(2,1)S(1)}, bf16[32,8,256]{2,1,0:T(8,128)(2,1)S(1)}, u32[]{:S(2)}, u32[]{:S(2)}) collective-permute-start(bf16[32,8,256]{2,1,0:T(8,128)(2,1)S(1)} %get-tuple-element.126), channel_id=1, source_target_pairs={{0,8},{8,0},{16,24},{24,16},{1,9},{9,1},{17,25},{25,17},{2,10},{10... | collective-permute-start | bytes 393224 | tf_op jit(solution)/shard_map/ppermute | solution.py:33
  59.0 24.2 %collective-permute-start.2 = (bf16[32,8,256]{2,1,0:T(8,128)(2,1)S(1)}, bf16[32,8,256]{2,1,0:T(8,128)(2,1)S(1)}, u32[]{:S(2)}, u32[]{:S(2)}) collective-permute-start(bf16[32,8,256]{2,1,0:T(8,128)(2,1)S(1)} %get-tuple-element.127), channel_id=1, source_target_pairs={{0,24},{8,16},{16,8},{24,0},{1,25},{9,17},{17,9},{25,1},{2,26},{10... | collective-permute-start | bytes 393224 | tf_op jit(solution)/shard_map/ppermute | solution.py:33
  71.1 8.3 %all-to-all-start.4 = ((bf16[4,2,128]{2,1,0:T(2,128)(2,1)}), bf16[4,2,128]{2,1,0:T(2,128)(2,1)S(1)}, u32[]{:S(2)}, u32[]{:S(2)}) async-start(bf16[4,2,128]{2,1,0:T(2,128)(2,1)} %reshape.302), calls=%async_computation.4 | async-start | bytes 4096 | tf_op jit(solution)/shard_map/all_to_all | solution.py:240
  79.4 10.2 %all-to-all-start.3 = ((bf16[32,32,256]{2,0,1:T(8,128)(2,1)}), bf16[32,32,256]{2,0,1:T(8,128)(2,1)S(1)}, u32[]{:S(2)}, u32[]{:S(2)}) async-start(bf16[32,32,256]{2,0,1:T(8,128)(2,1)} %copy.389), calls=%async_computation.3 | async-start | bytes 1048576 | tf_op jit(solution)/shard_map/all_to_all | solution.py:231
  83.9 7.0 %copy-start.11 = (bf16[4,32,8,256]{3,2,1,0:T(8,128)(2,1)}, bf16[4,32,8,256]{3,2,1,0:T(8,128)(2,1)S(1)}, u32[]{:S(2)}) copy-start(bf16[4,32,8,256]{3,2,1,0:T(8,128)(2,1)S(1)} %gather_fusion) | copy-start | bytes 1572868
  84.0 8.0 %copy-start.34 = (f32[256]{0:T(256)S(1)}, f32[256]{0:T(256)}, u32[]{:S(2)}) copy-start(f32[256]{0:T(256)} %param.18) | copy-start | bytes 3076
  92.3 0.8 copy-start.13
  100.2 5.8 %copy-start.16 = (bf16[128,8,256]{0,2,1:T(8,128)(2,1)}, bf16[128,8,256]{0,2,1:T(8,128)(2,1)S(1)}, u32[]{:S(2)}) copy-start(bf16[128,8,256]{0,2,1:T(8,128)(2,1)S(1)} %copy.397) | copy-start | bytes 1572868
  103.9 2.9 copy-start.21
  103.9 3.7 copy-start.33
  106.0 0.8 copy-start.2
  107.6 2.9 copy-start.6
  107.7 2.9 copy-start.38
  113.7 2.0 copy-start.7
  118.9 3.5 copy-start.17
  118.9 3.5 copy-start.18
  145.9 10.8 %all-to-all-start.5 = ((bf16[128,8,256]{2,1,0:T(8,128)(2,1)}), bf16[128,8,256]{2,1,0:T(8,128)(2,1)}, u32[]{:S(2)}, u32[]{:S(2)}) async-start(bf16[128,8,256]{2,1,0:T(8,128)(2,1)} %copy.411), calls=%async_computation.5 | async-start | bytes 1048576 | tf_op jit(solution)/shard_map/all_to_all | solution.py:254
  155.7 9.0 %copy-start.14 = (bf16[128,8,256]{2,0,1:T(8,128)(2,1)S(1)}, bf16[128,8,256]{2,0,1:T(8,128)(2,1)}, u32[]{:S(2)}) copy-start(bf16[128,8,256]{2,0,1:T(8,128)(2,1)} %copy-done.13) | copy-start | bytes 1572868
  158.6 18.8 %all-to-all-start.6 = ((bf16[32,32,256]{2,1,0:T(8,128)(2,1)}), bf16[32,32,256]{2,1,0:T(8,128)(2,1)S(1)}, u32[]{:S(2)}, u32[]{:S(2)}) async-start(bf16[32,32,256]{2,1,0:T(8,128)(2,1)} %bitcast.255), calls=%async_computation.6 | async-start | bytes 1048576 | tf_op jit(solution)/shard_map/all_to_all | solution.py:253
  162.1 200.5 %all-reduce.4.cloned.1.call-start = ((), (), s32[]{:S(2)}) async-start(), calls=%async_computation.8 | async-start | bytes 8388608 | tf_op jit(solution)/shard_map/psum | solution.py:265
  164.7 3.0 copy-start.8
  167.7 2.0 copy-start.12
  167.7 2.0 copy-start.39
  177.8 3.8 %copy-start.4 = (bf16[4,256,256]{1,2,0:T(8,128)(2,1)S(1)}, bf16[4,256,256]{1,2,0:T(8,128)(2,1)}, u32[]{:S(2)}) copy-start(bf16[4,256,256]{1,2,0:T(8,128)(2,1)} %copy-done.3) | copy-start | bytes 1572868
  181.6 2.7 copy-start.24
  184.4 8.0 %copy-start.26 = (bf16[4,256,256]{1,2,0:T(8,128)(2,1)S(1)}, bf16[4,256,256]{1,2,0:T(8,128)(2,1)}, u32[]{:S(2)}) copy-start(bf16[4,256,256]{1,2,0:T(8,128)(2,1)} %copy-done.25) | copy-start | bytes 1572868
  200.4 5.5 %copy-start.15 = (bf16[32,8,4,256]{3,1,2,0:T(8,128)(2,1)S(1)}, bf16[32,8,4,256]{3,1,2,0:T(8,128)(2,1)}, u32[]{:S(2)}) copy-start(bf16[32,8,4,256]{3,1,2,0:T(8,128)(2,1)} %copy.450) | copy-start | bytes 1572868
  200.4 6.5 %copy-start.10 = (bf16[4,256,256]{2,1,0:T(8,128)(2,1)S(1)}, bf16[4,256,256]{2,1,0:T(8,128)(2,1)}, u32[]{:S(2)}) copy-start(bf16[4,256,256]{2,1,0:T(8,128)(2,1)} %copy-done.9) | copy-start | bytes 1572868
  209.6 1.0 copy-start.27
  209.6 1.2 copy-start.28
  209.6 1.3 copy-start.30
  212.2 5.6 %copy-start.36 = (f32[256]{0:T(256)S(1)}, f32[256]{0:T(256)}, u32[]{:S(2)}) copy-start(f32[256]{0:T(256)} %get-tuple-element.73) | copy-start | bytes 3076
  212.2 5.6 %copy-start.37 = (f32[256]{0:T(256)S(1)}, f32[256]{0:T(256)}, u32[]{:S(2)}) copy-start(f32[256]{0:T(256)} %get-tuple-element.84) | copy-start | bytes 3076
  214.3 44.7 %all-to-all-start.7 = ((bf16[4,256,256]{2,0,1:T(4,128)(2,1)}), bf16[4,256,256]{2,0,1:T(4,128)(2,1)S(1)}, u32[]{:S(2)}, u32[]{:S(2)}) async-start(bf16[4,256,256]{2,0,1:T(4,128)(2,1)} %copy.421), calls=%async_computation.7 | async-start | bytes 1048576 | tf_op jit(solution)/shard_map/all_to_all | solution.py:263
  362.6 6.0 %copy-start.31 = (f32[256,256]{1,0:T(8,128)S(1)}, f32[256,256]{1,0:T(8,128)}, u32[]{:S(2)}) copy-start(f32[256,256]{1,0:T(8,128)} %get-tuple-element.147) | copy-start | bytes 786436
  362.6 6.7 %copy-start.20 = (f32[256,1024]{1,0:T(8,128)S(1)}, f32[256,1024]{1,0:T(8,128)}, u32[]{:S(2)}) copy-start(f32[256,1024]{1,0:T(8,128)} %get-tuple-element.149) | copy-start | bytes 3145732
  362.6 7.7 %copy-start.19 = (f32[1024,256]{1,0:T(8,128)S(1)}, f32[1024,256]{1,0:T(8,128)}, u32[]{:S(2)}) copy-start(f32[1024,256]{1,0:T(8,128)} %get-tuple-element.150) | copy-start | bytes 3145732
  364.8 6.4 %copy-start.1 = (bf16[256,1024]{1,0:T(8,128)(2,1)S(1)}, bf16[256,1024]{1,0:T(8,128)(2,1)}, u32[]{:S(2)}) copy-start(bf16[256,1024]{1,0:T(8,128)(2,1)} %param.22) | copy-start | bytes 1572868
Sparse Core Ops, SparseCore 0:
  209.8 152.8 all-reduce.3
